TPU v7x, 256 devices: a whole 4x4x8 slice. The times are simulated.
256 devices in a mesh: row: 16 (over z, core), col: 16 (over x, y).
Axes of the slice: x: 4, y: 4, z: 8, core: 2. Of those that a mesh axis runs over, the one named last changes fastest.
Arguments:
- panel: float32 [16384, 128], P(('row', 'col')), as said below
- mobility: float32 [16384, 16384], P('row', 'col'), as said below
Outputs:
- updated: float32 [16384, 16384], P('row', 'col')
- panel_factor: float32 [128, 128], replicated
Inputs may be any that keep to these rules, and one draw needn't show every extreme that they name: Each row and each column of the panel has its own scale. `mobility`: Symmetric.
All inputs are finite; a program needn't handle non-finite values.
Results may differ from a plain program's by a relative error of at most 0.000076.
Values sent between devices are 32-bit elements; how exact they have to be, the bound alone decides.
No kernel may reach another device: no remote copies, remote signals or barrier semaphores. Data moves between devices by JAX's collectives and lax.ppermute only.
A program may use at most 64 MiB of HBM per device.

v0:
```python
import jax
import jax.numpy as jnp
from jax import lax
from jax.sharding import PartitionSpec as P


def spread(shard, axis, root):
    mine = lax.axis_index(axis) == root
    return lax.psum(jnp.where(mine, shard, jnp.zeros_like(shard)), axis)


def product(first_op, second_op):
    return jnp.dot(
        first_op, second_op, precision=lax.Precision.HIGHEST, preferred_element_type=jnp.float32
    )


def product_tn(first_op, second_op):
    return lax.dot_general(
        first_op,
        second_op,
        (((0,), (0,)), ((), ())),
        precision=lax.Precision.HIGHEST,
        preferred_element_type=jnp.float32,
    )


def product_nt(first_op, second_op):
    return lax.dot_general(
        first_op,
        second_op,
        (((1,), (1,)), ((), ())),
        precision=lax.Precision.HIGHEST,
        preferred_element_type=jnp.float32,
    )


def invert_core(core_matrix):
    identity = jnp.eye(core_matrix.shape[0], dtype=jnp.float32)

    def newton_step(index, approx):
        return product(approx, 2.0 * identity - product(core_matrix, approx))

    return lax.fori_loop(0, 12, newton_step, identity)


def correction_columns(block_rows_arr, block_ratio):
    root_index = lax.axis_index("col") * block_ratio + 0
    copies = spread(block_rows_arr, "row", root_index)
    return copies


def on_device(panel, mobility):
    piece_rows = panel.shape[0]
    width_cols = panel.shape[1]
    count_col = lax.axis_size("col")
    count_row = lax.axis_size("row")
    block_ratio = count_row // count_col
    row_index = lax.axis_index("row")
    col_index = lax.axis_index("col")
    block_rows = mobility.shape[0]
    block_cols = mobility.shape[1]
    first_row = (row_index * count_col + col_index) * piece_rows
    positions = first_row + jnp.arange(piece_rows, dtype=jnp.int32)
    selector = (jnp.arange(width_cols, dtype=jnp.int32)[:, None] == positions[None, :]).astype(
        jnp.float32
    )
    gram_term = product_tn(panel, panel)
    top_term = product(selector, panel)
    gram_sum, top_rows = lax.psum((gram_term, top_term), ("row", "col"))
    lower_factor = jnp.linalg.cholesky(gram_sum)
    panel_factor = lower_factor.T
    ortho_piece = jax.scipy.linalg.solve_triangular(lower_factor, panel.T, lower=True).T
    basis_piece = ortho_piece + selector.T
    top_ortho = jax.scipy.linalg.solve_triangular(lower_factor, top_rows.T, lower=True)
    core_matrix = jnp.eye(width_cols, dtype=jnp.float32) + top_ortho
    kernel = invert_core(core_matrix)
    everything = lax.all_gather(basis_piece, ("row", "col"), axis=0, tiled=True)
    basis_rows = lax.dynamic_slice_in_dim(everything, row_index * block_rows, block_rows, 0)
    basis_cols = lax.dynamic_slice_in_dim(everything, col_index * block_cols, block_cols, 0)
    partial_rows = product(mobility, basis_cols)
    spread_rows = product(lax.psum(partial_rows, "col"), kernel)
    inner_sum = lax.psum(product_tn(basis_rows, spread_rows), "row")
    inner = product_tn(kernel, inner_sum)
    correction_rows = spread_rows - 0.5 * product(basis_rows, inner)
    correction_cols = correction_columns(correction_rows, block_ratio)
    left_side = jnp.concatenate([basis_rows, correction_rows], axis=1)
    right_side = jnp.concatenate([correction_cols, basis_cols], axis=1)
    updated = mobility - product_nt(left_side, right_side)
    return (updated, panel_factor)


def solution(mesh):
    in_specs = (P(("row", "col"), None), P("row", "col"))
    out_specs = (P("row", "col"), P())
    return jax.shard_map(
        on_device, mesh=mesh, in_specs=in_specs, out_specs=out_specs, check_vma=False
    )
```

profile of v0, /device:TPU:1, one launch (start us, length us, event | category | flops | bytes accessed | tf_op | source)
XLA Modules:
  0.0 727.7 jit_solution(3753922273948830282)
XLA Ops:
  7.2 0.0 copy-start
  7.2 0.0 all-reduce.12.cloned.1.call-start
  7.2 0.7 copy-done
  7.9 0.9 fusion.18
  8.8 0.8 fusion.14
  9.6 0.0 all-reduce.12.cloned.1.call-update
  9.7 0.0 all-gather.2.cloned.1.call-start
  9.7 249.4 %all-reduce.12.cloned.1.call-done = (f32[128,128]{0,1:T(8,128)}, f32[128,128]{1,0:T(8,128)}) async-done(((f32[128,128]{0,1:T(8,128)}, f32[128,128]{1,0:T(8,128)}), (f32[128,128]{0,1:T(8,128)}, f32[128,128]{1,0:T(8,128)})) %all-reduce.12.cloned.1.call-update) | async-done | bytes 131088 | tf_op jit(solution)/shard_map/psum | solution.py:70
  259.1 0.9 copy.5
  260.0 0.9 fusion.12
  260.9 11.7 %cholesky.19 = f32[128,128]{1,0:T(8,128)S(1)} custom-call(f32[128,128]{1,0:T(8,128)S(1)} %fusion.12), custom_call_target="Cholesky" | custom-call | tf_op jit(solution)/shard_map/jit(cholesky)/cholesky | solution.py:71
  272.6 0.6 compare_reduce_fusion
  273.3 0.7 fusion.15
  273.9 9.8 %custom-call.10 = f32[1,128,128]{1,2,0:T(8,128)S(1)} custom-call(f32[1,128,128]{2,1,0:T(8,128)S(1)} %get-tuple-element.49), custom_call_target="InvertDiagBlocksLowerTriangular" | custom-call | tf_op jit(solution)/shard_map/jit(_solve_triangular)/triangular_solve | solution.py:73
  283.8 0.8 fusion.3
  284.6 0.0 all-gather.2.cloned.1.call-update
  284.6 0.0 all-reduce.6.cloned.1.call-start
  284.7 0.1 copy.6
  284.7 1.1 convolution_add_fusion
  285.9 115.3 %all-gather.2.cloned.1.call-done = f32[16384,128]{1,0:T(8,128)} async-done(((f32[64,128]{1,0:T(8,128)}), f32[16384,128]{1,0:T(8,128)}) %all-gather.2.cloned.1.call-update) | async-done | bytes 8388624 | tf_op jit(solution)/shard_map/all_gather | solution.py:78
  401.2 1.3 constant_dynamic-slice_fusion.1
  402.5 7.5 %convolution_bitcast_fusion.1 = f32[1024,128]{0,1:T(8,128)} fusion(f32[1024,128]{1,0:T(8,128)S(1)} %get-tuple-element.47, f32[1024,1024]{1,0:T(8,128)} %param.5), kind=kOutput, calls=%fused_computation.7 | convolution fusion | flops 1610612736 | bytes 5242880 | tf_op jit(solution)/shard_map/dot_general | solution.py:13
  409.9 0.0 all-reduce.6.cloned.1.call-update
  410.0 0.2 all-reduce.8.cloned.1.call-start
  410.2 7.1 while.11
  410.2 0.3 convolution_subtract_fusion.3
  410.5 0.3 convolution_bitcast_fusion.4
  410.8 0.3 convolution_subtract_fusion.3
  411.1 0.3 convolution_bitcast_fusion.4
  411.4 0.3 convolution_subtract_fusion.3
  411.7 0.3 convolution_bitcast_fusion.4
  412.0 0.3 convolution_subtract_fusion.3
  412.3 0.3 convolution_bitcast_fusion.4
  412.6 0.3 convolution_subtract_fusion.3
  412.9 0.3 convolution_bitcast_fusion.4
  413.2 0.3 convolution_subtract_fusion.3
  413.5 0.3 convolution_bitcast_fusion.4
  413.8 0.3 convolution_subtract_fusion.3
  414.0 0.3 convolution_bitcast_fusion.4
  414.4 0.3 convolution_subtract_fusion.3
  414.6 0.3 convolution_bitcast_fusion.4
  415.0 0.3 convolution_subtract_fusion.3
  415.2 0.3 convolution_bitcast_fusion.4
  415.6 0.3 convolution_subtract_fusion.3
  415.8 0.3 convolution_bitcast_fusion.4
  416.1 0.3 convolution_subtract_fusion.3
  416.4 0.3 convolution_bitcast_fusion.4
  416.7 0.3 convolution_subtract_fusion.3
  417.0 0.3 convolution_bitcast_fusion.4
  417.3 83.1 %all-reduce.6.cloned.1.call-done = f32[1024,128]{0,1:T(8,128)} async-done(((f32[1024,128]{0,1:T(8,128)}), f32[1024,128]{0,1:T(8,128)}) %all-reduce.6.cloned.1.call-update) | async-done | bytes 524304 | tf_op jit(solution)/shard_map/psum | solution.py:82
  500.4 1.6 fusion.19
  502.1 1.6 fusion.20
  503.7 0.0 all-reduce.8.cloned.1.call-update
  503.7 0.0 all-reduce.10.cloned.1.call-start
  503.8 0.2 copy.8
  504.0 99.9 %all-reduce.8.cloned.1.call-done = f32[128,128]{1,0:T(8,128)} async-done(((f32[128,128]{1,0:T(8,128)}), f32[128,128]{1,0:T(8,128)}) %all-reduce.8.cloned.1.call-update) | async-done | bytes 65552 | tf_op jit(solution)/shard_map/psum | solution.py:83
  603.9 1.0 fusion.21
  604.9 1.4 broadcast_select_fusion
  606.3 0.0 all-reduce.10.cloned.1.call-update
  606.3 0.7 copy.9
  607.1 107.4 %all-reduce.10.cloned.1.call-done = f32[1024,128]{1,0:T(8,128)} async-done(((f32[1024,128]{1,0:T(8,128)}), f32[1024,128]{1,0:T(8,128)}) %all-reduce.10.cloned.1.call-update) | async-done | bytes 524304 | tf_op jit(solution)/shard_map/psum | solution.py:9
  714.4 6.7 convolution_subtract_fusion.1
  (15 shorter events, 0.1 us)
Async XLA Ops:
  7.2 0.8 copy-start
  7.2 251.9 %all-reduce.12.cloned.1.call-start = ((), (), s32[]{:S(2)}) async-start(), calls=%async_computation.4 | async-start | bytes 262144 | tf_op jit(solution)/shard_map/psum | solution.py:70
  9.7 391.5 %all-gather.2.cloned.1.call-start = ((), (), s32[]{:S(2)}) async-start(), calls=%async_computation | async-start | bytes 8421376 | tf_op jit(solution)/shard_map/all_gather | solution.py:78
  284.6 215.8 %all-reduce.6.cloned.1.call-start = ((), (), s32[]{:S(2)}) async-start(), calls=%async_computation.1 | async-start | bytes 1048576 | tf_op jit(solution)/shard_map/psum | solution.py:82
  410.0 193.9 %all-reduce.8.cloned.1.call-start = ((), (), s32[]{:S(2)}) async-start(), calls=%async_computation.2 | async-start | bytes 131072 | tf_op jit(solution)/shard_map/psum | solution.py:83
  503.7 210.7 %all-reduce.10.cloned.1.call-start = ((), (), s32[]{:S(2)}) async-start(), calls=%async_computation.3 | async-start | bytes 1048576 | tf_op jit(solution)/shard_map/psum | solution.py:9
Sparse Core Ops, SparseCore 0:
  14.2 244.8 all-reduce.11
  284.7 116.4 all-gather.1
  410.1 90.2 all-reduce.5
  503.8 99.9 all-reduce.7
  606.6 107.7 all-reduce.9
where the time goes:
time: 728 us
  waiting for transfers between devices  655 us (90%)
  matrix products  30.2 us (4%)
  other arithmetic  23.7 us (3%)
  between operations  13.9 us (2%)
    psum x1, waiting for transfers between devices, on_device(): gram_sum, top_rows = lax.psum((gram_term, top_term), ('row', 'col'))  249 us
    all_gather x1, waiting for transfers between devices, on_device(): everything = lax.all_gather(basis_piece, ('row', 'col'), axis=0, tiled=True)  115 us
    psum x1, waiting for transfers between devices, spread(): return lax.psum(jnp.where(mine, shard, jnp.zeros_like(shard)), axis)  107 us
    psum x1, waiting for transfers between devices, on_device(): inner_sum = lax.psum(product_tn(basis_rows, spread_rows), 'row')  99.9 us
    psum x1, waiting for transfers between devices, on_device(): spread_rows = product(lax.psum(partial_rows, 'col'), kernel)  83.1 us
    dot_general x28, matrix products, product(): jnp.dot(first_op, second_op, precision=lax.Precision.HIGHEST, preferred_e...  17.9 us
  transfers between devices with their start and end apart: 5, of which 5 were waited for; matrix products, arithmetic and copies ran while one was open for 1% of the time, Pallas kernels for 0%

commit v1 on v0

--- a/solution.py
+++ b/solution.py
@@ -75,7 +75,12 @@
     top_ortho = jax.scipy.linalg.solve_triangular(lower_factor, top_rows.T, lower=True)
     core_matrix = jnp.eye(width_cols, dtype=jnp.float32) + top_ortho
     kernel = invert_core(core_matrix)
-    everything = lax.all_gather(basis_piece, ("row", "col"), axis=0, tiled=True)
+    everything = jnp.concatenate(
+        lax.all_to_all(
+            jnp.stack([basis_piece] * lax.axis_size(("row", "col"))), ("row", "col"), 0, 0
+        ),
+        axis=0,
+    )
     basis_rows = lax.dynamic_slice_in_dim(everything, row_index * block_rows, block_rows, 0)
     basis_cols = lax.dynamic_slice_in_dim(everything, col_index * block_cols, block_cols, 0)
     partial_rows = product(mobility, basis_cols)

time: 728 us -> 811 us (1.11)
  waiting for transfers between devices: 655 us -> 724 us
  starting transfers between devices: 0.39 us -> 10.9 us
    all_to_all x0 -> x1, waiting for transfers between devices: none -> 185 us  [on_device(): lax.all_to_all(jnp.stack([basis_piece] * lax.axis_size(('row', 'col'))),...]
    all_gather x1 -> x0, waiting for transfers between devices: 115 us -> none  [on_device(): everything = lax.all_gather(basis_piece, ('row', 'col'), axis=0, tiled=True)]
    all_to_all x0 -> x1, starting transfers between devices: none -> 10.6 us  [on_device(): lax.all_to_all(jnp.stack([basis_piece] * lax.axis_size(('row', 'col'))),...]
where the time goes in v1:
time: 811 us
  waiting for transfers between devices  724 us (89%)
  matrix products  28.8 us (4%)
  other arithmetic  23.7 us (3%)
  between operations  13.9 us (2%)
  starting transfers between devices  10.9 us (1%)
  local copies, waits for them, and re-layouts  8.45 us (1%)
    psum x1, waiting for transfers between devices, on_device(): gram_sum, top_rows = lax.psum((gram_term, top_term), ('row', 'col'))  249 us
    all_to_all x1, waiting for transfers between devices, on_device(): lax.all_to_all(jnp.stack([basis_piece] * lax.axis_size(('row', 'col'))),...  185 us
    psum x1, waiting for transfers between devices, spread(): return lax.psum(jnp.where(mine, shard, jnp.zeros_like(shard)), axis)  107 us
    psum x1, waiting for transfers between devices, on_device(): inner_sum = lax.psum(product_tn(basis_rows, spread_rows), 'row')  100 us
    psum x1, waiting for transfers between devices, on_device(): spread_rows = product(lax.psum(partial_rows, 'col'), kernel)  83 us
    dot_general x28, matrix products, product(): jnp.dot(first_op, second_op, precision=lax.Precision.HIGHEST, preferred_e...  18 us
  transfers between devices with their start and end apart: 5, of which 5 were waited for; matrix products, arithmetic and copies ran while one was open for 1% of the time, Pallas kernels for 0%

profile of v1, /device:TPU:1, one launch (start us, length us, event | category | flops | bytes accessed | tf_op | source)
XLA Modules:
  0.0 810.6 jit_solution(15237412350434089871)
XLA Ops:
  7.2 0.0 copy-start
  7.2 0.0 all-reduce.12.cloned.1.call-start
  7.2 0.7 copy-done
  7.9 0.9 fusion.18
  8.8 0.8 fusion.14
  9.6 0.0 all-reduce.12.cloned.1.call-update
  9.7 249.4 %all-reduce.12.cloned.1.call-done = (f32[128,128]{0,1:T(8,128)}, f32[128,128]{1,0:T(8,128)}) async-done(((f32[128,128]{0,1:T(8,128)}, f32[128,128]{1,0:T(8,128)}), (f32[128,128]{0,1:T(8,128)}, f32[128,128]{1,0:T(8,128)})) %all-reduce.12.cloned.1.call-update) | async-done | bytes 131088 | tf_op jit(solution)/shard_map/psum | solution.py:70
  259.1 0.9 copy.10
  260.0 0.9 fusion.12
  260.9 11.7 %cholesky.19 = f32[128,128]{1,0:T(8,128)S(1)} custom-call(f32[128,128]{1,0:T(8,128)S(1)} %fusion.12), custom_call_target="Cholesky" | custom-call | tf_op jit(solution)/shard_map/jit(cholesky)/cholesky | solution.py:71
  272.6 0.6 compare_reduce_fusion
  273.3 0.7 fusion.15
  273.9 9.8 %custom-call.10 = f32[1,128,128]{1,2,0:T(8,128)S(1)} custom-call(f32[1,128,128]{2,1,0:T(8,128)S(1)} %get-tuple-element.54), custom_call_target="InvertDiagBlocksLowerTriangular" | custom-call | tf_op jit(solution)/shard_map/jit(_solve_triangular)/triangular_solve | solution.py:73
  283.8 0.2 fusion.3
  283.9 4.3 stack.2
  288.2 10.6 %all-to-all-start = ((f32[256,64,128]{2,1,0:T(8,128)}), f32[256,64,128]{2,1,0:T(8,128)}, u32[]{:S(2)}, u32[]{:S(2)}) async-start(f32[256,64,128]{2,1,0:T(8,128)} %stack.2), calls=%async_computation | async-start | bytes 16777216 | tf_op jit(solution)/shard_map/all_to_all | solution.py:79
  298.8 0.2 all-reduce.6.cloned.1.call-start
  299.1 0.1 copy.13
  299.2 0.0 copy-done.1
  299.2 0.3 convolution_add_fusion
  299.5 185.0 %all-to-all-done = f32[256,64,128]{2,1,0:T(8,128)} async-done(((f32[256,64,128]{2,1,0:T(8,128)}), f32[256,64,128]{2,1,0:T(8,128)}, u32[]{:S(2)}, u32[]{:S(2)}) %all-to-all-start) | async-done | bytes 8388640 | tf_op jit(solution)/shard_map/all_to_all | solution.py:79
  484.4 1.3 constant_dynamic-slice_fusion.1
  485.7 7.5 convolution_bitcast_fusion.1
  493.2 0.0 all-reduce.6.cloned.1.call-update
  493.2 0.0 all-reduce.8.cloned.1.call-start
  493.2 7.1 while.11
  493.3 0.3 convolution_subtract_fusion.3
  493.5 0.3 convolution_bitcast_fusion.4
  493.9 0.3 convolution_subtract_fusion.3
  494.1 0.3 convolution_bitcast_fusion.4
  494.5 0.3 convolution_subtract_fusion.3
  494.7 0.3 convolution_bitcast_fusion.4
  495.1 0.3 convolution_subtract_fusion.3
  495.3 0.3 convolution_bitcast_fusion.4
  495.6 0.3 convolution_subtract_fusion.3
  495.9 0.3 convolution_bitcast_fusion.4
  496.2 0.3 convolution_subtract_fusion.3
  496.5 0.3 convolution_bitcast_fusion.4
  496.8 0.3 convolution_subtract_fusion.3
  497.1 0.3 convolution_bitcast_fusion.4
  497.4 0.3 convolution_subtract_fusion.3
  497.7 0.3 convolution_bitcast_fusion.4
  498.0 0.3 convolution_subtract_fusion.3
  498.3 0.3 convolution_bitcast_fusion.4
  498.6 0.3 convolution_subtract_fusion.3
  498.9 0.3 convolution_bitcast_fusion.4
  499.2 0.3 convolution_subtract_fusion.3
  499.5 0.3 convolution_bitcast_fusion.4
  499.8 0.3 convolution_subtract_fusion.3
  500.1 0.3 convolution_bitcast_fusion.4
  500.4 83.0 %all-reduce.6.cloned.1.call-done = f32[1024,128]{0,1:T(8,128)} async-done(((f32[1024,128]{0,1:T(8,128)}), f32[1024,128]{0,1:T(8,128)}) %all-reduce.6.cloned.1.call-update) | async-done | bytes 524304 | tf_op jit(solution)/shard_map/psum | solution.py:87
  583.4 1.6 fusion.19
  585.0 1.6 fusion.20
  586.6 0.0 all-reduce.8.cloned.1.call-update
  586.7 0.0 all-reduce.10.cloned.1.call-start
  586.7 100.1 %all-reduce.8.cloned.1.call-done = f32[128,128]{1,0:T(8,128)} async-done(((f32[128,128]{1,0:T(8,128)}), f32[128,128]{1,0:T(8,128)}) %all-reduce.8.cloned.1.call-update) | async-done | bytes 65552 | tf_op jit(solution)/shard_map/psum | solution.py:88
  686.8 1.0 fusion.21
  687.9 1.4 broadcast_select_fusion
  689.3 0.0 all-reduce.10.cloned.1.call-update
  689.4 0.7 copy.14
  690.1 0.2 copy.17
  690.3 0.2 copy.16
  690.5 106.9 %all-reduce.10.cloned.1.call-done = f32[1024,128]{0,1:T(8,128)} async-done(((f32[1024,128]{0,1:T(8,128)}), f32[1024,128]{0,1:T(8,128)}) %all-reduce.10.cloned.1.call-update) | async-done | bytes 524304 | tf_op jit(solution)/shard_map/psum | solution.py:9
  797.4 6.7 convolution_subtract_fusion.1
  (16 shorter events, 0.1 us)
Async XLA Ops:
  7.2 0.8 copy-start
  7.2 251.9 %all-reduce.12.cloned.1.call-start = ((), (), s32[]{:S(2)}) async-start(), calls=%async_computation.4 | async-start | bytes 262144 | tf_op jit(solution)/shard_map/psum | solution.py:70
  288.2 11.0 %copy-start.1 = (f32[128,128]{1,0:T(8,128)S(1)}, f32[128,128]{1,0:T(8,128)}, u32[]{:S(2)}) copy-start(f32[128,128]{1,0:T(8,128)} %get-tuple-element.50) | copy-start | bytes 196612
  288.2 196.2 %all-to-all-start = ((f32[256,64,128]{2,1,0:T(8,128)}), f32[256,64,128]{2,1,0:T(8,128)}, u32[]{:S(2)}, u32[]{:S(2)}) async-start(f32[256,64,128]{2,1,0:T(8,128)} %stack.2), calls=%async_computation | async-start | bytes 16777216 | tf_op jit(solution)/shard_map/all_to_all | solution.py:79
  298.8 284.5 %all-reduce.6.cloned.1.call-start = ((), (), s32[]{:S(2)}) async-start(), calls=%async_computation.1 | async-start | bytes 1048576 | tf_op jit(solution)/shard_map/psum | solution.py:87
  493.2 193.6 %all-reduce.8.cloned.1.call-start = ((), (), s32[]{:S(2)}) async-start(), calls=%async_computation.2 | async-start | bytes 131072 | tf_op jit(solution)/shard_map/psum | solution.py:88
  586.7 210.7 %all-reduce.10.cloned.1.call-start = ((), (), s32[]{:S(2)}) async-start(), calls=%async_computation.3 | async-start | bytes 1048576 | tf_op jit(solution)/shard_map/psum | solution.py:9
Sparse Core Ops, SparseCore 0:
  14.2 244.8 all-reduce.11
  493.3 90.0 all-reduce.5
  586.8 100.0 all-reduce.7
  689.6 107.7 all-reduce.9
